TPU v7x, 32 devices: a whole 2x2x4 slice. The times are simulated.
32 devices in a mesh: groups: 2 (over y), ctx: 4 (over z), head: 4 (over x, core).
Axes of the slice: x: 2, y: 2, z: 4, core: 2. Of those that a mesh axis runs over, the one named last changes fastest.
Arguments:
- queries: bfloat16 [1024, 32, 128], P(('groups', 'ctx'), 'head'), parts along dimension 0, may hold values from -16 to 16
- positions: int32 [1024], P(('groups', 'ctx')), parts along dimension 0, may hold values from 4096 to 6143
- key_codes: bfloat16 [4, 4096, 128], P('groups', 'ctx'), parts along dimension 0, may hold values from -16 to 16
- value_codes: bfloat16 [4, 4096, 128], P('groups', 'ctx'), parts along dimension 0, may hold values from -8 to 8
- scale_index: int32 [4, 2, 32], P('groups', None, 'ctx'), parts along dimension 0, may hold values from 0 to 15
- scale_table: float32 [2, 16], replicated, may hold values from 0.5 to 2
- block_lists: int32 [64, 4, 8], P(('groups', 'head')), parts along dimension 0, may hold values from 0 to 31, as said below
Outputs:
- attended: bfloat16 [1024, 4096], P(('groups', 'ctx', 'head')), parts along dimension 0
There are 2 independent parts, one for each index of `groups`. A program takes and returns all parts, laid end to end along the dimension named above; an argument that names none is the same for every part. Nothing has to cross between parts.
Inputs may be any that keep to these rules, and one draw needn't show every extreme that they name: For query head h and query block b, block_lists[h, b, :] names 8 different key blocks. Call the rows of b's index of ctx (a run of 128 rows) its shard c; every listed block lies on a key shard (a run of 1024 keys) at most 1 shards from c counted around the closed cycle of key shards in either direction, and at least one listed block lies exactly 1 shards away.
All inputs are finite; a program needn't handle non-finite values.
Results may differ from a plain program's by a relative error of at most 0.0065.
The roundings to bfloat16 on the way count: a program that leaves them out, or rounds other values in their place, can miss the bound.
Values may be sent and summed in bfloat16 or wider, within the bound.
A program may use at most 64 MiB of HBM per device.

v0:
```python
import functools
import math

import jax
import jax.numpy as jnp
import numpy as np
from jax import lax
from jax.experimental import pallas as pl
from jax.experimental.pallas import tpu as pltpu
from jax.sharding import PartitionSpec as P

GROUP = 16
BLOCK = 128
ROPE_BASE = 500000.0
PIECES = 1
CUTS = 1
MESH = pl.DeviceIdType.MESH


def attend(
    reach, n_ctx, n_head,
    lists_hbm, index_hbm, table_hbm, pos_hbm, freq_hbm, q_hbm, k_hbm, v_hbm,
    out_ref,
    lists_s, index_s, table_s, pos_ref, freq_ref,
    qcode, kcode, vcode, qwide, qrot, kbuf, vbuf, wbuf, lbuf, obuf,
    load_sem, ksend, krecv, vsend, vrecv, kfs, kfr, vfs, vfr, osend, orecv, own_sem,
):
    c = lax.axis_index("ctx")
    hp = lax.axis_index("head")
    heads, rows, dh = qrot.shape
    keys = kcode.shape[0]
    kblocks = keys // BLOCK
    nsel = lists_s.shape[2]
    rows_per = out_ref.shape[0]
    slots = 2 * reach + 1
    half = lax.rem(hp, 2)
    sib = hp + 1 - 2 * half
    kv_head = hp * heads // GROUP

    barrier = pltpu.get_barrier_semaphore()
    offsets = [o for d in range(1, reach + 1) for o in (d, -d)]
    for o in offsets:
        pl.semaphore_signal(
            barrier, inc=1, device_id={"ctx": lax.rem(c + o + n_ctx, n_ctx)}, device_id_type=MESH
        )
    for k in range(1, n_head):
        pl.semaphore_signal(
            barrier, inc=1, device_id={"head": lax.rem(hp + k, n_head)}, device_id_type=MESH
        )

    k_load = pltpu.make_async_copy(k_hbm.at[kv_head], kcode, load_sem.at[0])
    v_load = pltpu.make_async_copy(v_hbm.at[kv_head], vcode, load_sem.at[1])
    q_load = pltpu.make_async_copy(q_hbm, qcode, load_sem.at[2])
    small = [
        pltpu.make_async_copy(src, dst, load_sem.at[3 + i])
        for i, (src, dst) in enumerate(
            [
                (index_hbm, index_s),
                (table_hbm, table_s),
                (lists_hbm, lists_s),
                (pos_hbm, pos_ref),
                (freq_hbm, freq_ref),
            ]
        )
    ]
    k_load.start()
    for copy in small[:2]:
        copy.start()
    v_load.start()
    q_load.start()
    for copy in small[2:]:
        copy.start()

    own = reach * kblocks
    for copy in small[:2]:
        copy.wait()
    k_load.wait()
    for b in range(kblocks):
        s = table_s[0, index_s[0, kv_head, b]]
        kbuf[own + b] = (kcode[b * BLOCK : (b + 1) * BLOCK, :].astype(jnp.float32) * s).astype(
            jnp.bfloat16
        )

    part = kblocks // 2 // PIECES
    cuts = vsend.shape[1]
    wide = dh // cuts

    def k_copy(o, piece):
        return pltpu.make_async_remote_copy(
            src_ref=kbuf.at[pl.ds(own + half * (kblocks // 2) + piece * part, part)],
            dst_ref=kbuf.at[
                pl.ds((reach - o) * kblocks + half * (kblocks // 2) + piece * part, part)
            ],
            send_sem=ksend.at[reach - o, piece],
            recv_sem=krecv.at[reach - o, piece],
            device_id={"ctx": lax.rem(c + o + n_ctx, n_ctx)},
            device_id_type=MESH,
        )

    def v_copy(o, piece):
        return pltpu.make_async_remote_copy(
            src_ref=vbuf.at[pl.ds(own + half * (kblocks // 2), kblocks // 2), pl.ds(piece * wide, wide)],
            dst_ref=vbuf.at[
                pl.ds((reach - o) * kblocks + half * (kblocks // 2), kblocks // 2),
                pl.ds(piece * wide, wide),
            ],
            send_sem=vsend.at[reach - o, piece],
            recv_sem=vrecv.at[reach - o, piece],
            device_id={"ctx": lax.rem(c + o + n_ctx, n_ctx)},
            device_id_type=MESH,
        )

    def k_forward(slot, piece, which):
        region = kbuf.at[pl.ds(slot * kblocks + which * (kblocks // 2) + piece * part, part)]
        return forward(region, kfs, kfr, slot, piece)

    def v_forward(slot, piece, which):
        region = vbuf.at[
            pl.ds(slot * kblocks + which * (kblocks // 2), kblocks // 2), pl.ds(piece * wide, wide)
        ]
        return forward(region, vfs, vfr, slot, piece)

    def forward(region, send, recv, slot, piece):
        return pltpu.make_async_remote_copy(
            src_ref=region,
            dst_ref=region,
            send_sem=send.at[slot, piece],
            recv_sem=recv.at[slot, piece],
            device_id={"head": sib},
            device_id_type=MESH,
        )

    pl.semaphore_wait(barrier, len(offsets) + n_head - 1)
    for piece in range(PIECES):
        for o in offsets:
            k_copy(o, piece).start()

    v_load.wait()
    for b in range(kblocks):
        s = table_s[1, index_s[1, kv_head, b]]
        rounded = (vcode[b * BLOCK : (b + 1) * BLOCK, :].astype(jnp.float32) * s).astype(jnp.bfloat16)
        vbuf[own + b] = rounded.astype(jnp.float32).T.astype(jnp.bfloat16)
    for piece in range(cuts):
        for o in offsets:
            v_copy(o, piece).start()

    q_load.wait()
    for copy in small[2:]:
        copy.wait()
    qwide[...] = qcode[...].astype(jnp.float32)
    pos = jnp.broadcast_to(pos_ref[...].astype(jnp.float32), (rows, rows)).T
    angle = pos * freq_ref[...]
    lane = lax.broadcasted_iota(jnp.int32, (rows, dh), 1)
    even = lax.rem(lane, 2) == 0
    cosine = jnp.cos(angle)
    sine = jnp.sin(angle)
    sine = jnp.where(even, -sine, sine)
    for h in range(heads):
        x = qwide[pl.ds(h, rows, stride=heads), :]
        other = jnp.where(even, pltpu.roll(x, dh - 1, 1), pltpu.roll(x, 1, 1))
        qrot[h] = (x * cosine + other * sine).astype(jnp.bfloat16)

    for piece in range(PIECES):
        for o in offsets:
            k_copy(o, piece).wait_recv()
            k_forward(reach - o, piece, half).start()
    for piece in range(PIECES):
        for o in offsets:
            k_forward(reach - o, piece, 1 - half).wait_recv()

    total = n_ctx * kblocks
    base = total - (c - reach) * kblocks
    factor = math.log2(math.e) / math.sqrt(dh)

    def block_of(h, j):
        return jnp.minimum(lax.rem(lists_s[h, c, j] + base, total), slots * kblocks - 1)

    def score(h, carry):
        gathered = jnp.concatenate([kbuf[block_of(h, j)] for j in range(nsel)], axis=0)
        s = lax.dot_general(
            gathered, qrot[h], (((1,), (1,)), ((), ())), preferred_element_type=jnp.float32
        )
        m = jnp.max(s, axis=0, keepdims=True)
        w = jnp.exp2((s - m) * factor)
        lbuf[h] = 1.0 / jnp.sum(w, axis=0, keepdims=True)
        wbuf[h] = w.astype(jnp.bfloat16)
        return carry

    lax.fori_loop(0, heads, score, 0, unroll=True)

    def columns(h):
        return pl.ds(pl.multiple_of((hp * heads + h) * dh, dh), dh)

    def o_copy(h, k):
        peer = lax.rem(hp + k, n_head)
        return pltpu.make_async_remote_copy(
            src_ref=obuf.at[h, peer],
            dst_ref=out_ref.at[:, columns(h)],
            send_sem=osend.at[h, k - 1],
            recv_sem=orecv.at[h, k - 1],
            device_id={"head": peer},
            device_id_type=MESH,
        )

    def own_copy(h):
        return pltpu.make_async_copy(obuf.at[h, hp], out_ref.at[:, columns(h)], own_sem.at[h])

    def value(h, carry):
        gathered = jnp.concatenate([vbuf[block_of(h, j)] for j in range(nsel)], axis=1)
        o = jnp.dot(gathered, wbuf[h], preferred_element_type=jnp.float32)
        t = (o * lbuf[h]).T
        for p in range(n_head):
            obuf[h, p] = t[p * rows_per : (p + 1) * rows_per, :].astype(jnp.bfloat16)
        for k in range(1, n_head):
            o_copy(h, k).start()
        own_copy(h).start()
        return carry

    for piece in range(cuts):
        for o in offsets:
            v_copy(o, piece).wait_recv()
            v_forward(reach - o, piece, half).start()
    for piece in range(cuts):
        for o in offsets:
            v_forward(reach - o, piece, 1 - half).wait_recv()
    lax.fori_loop(0, heads, value, 0, unroll=True)

    for o in offsets:
        for piece in range(PIECES):
            k_copy(o, piece).wait_send()
            k_forward(reach - o, piece, half).wait_send()
        for piece in range(cuts):
            v_copy(o, piece).wait_send()
            v_forward(reach - o, piece, half).wait_send()

    def finish(h, carry):
        own_copy(h).wait()
        for k in range(1, n_head):
            o_copy(h, k).wait()
        return carry

    lax.fori_loop(0, heads, finish, 0)


def on_device(queries, positions, key_codes, value_codes, scale_index, scale_table, block_lists):
    n_ctx = lax.axis_size("ctx")
    n_head = lax.axis_size("head")
    reach = min(3, (n_ctx - 1) // 2)
    rows, heads, dh = queries.shape
    keys = key_codes.shape[1]
    kblocks = keys // BLOCK
    nsel = block_lists.shape[2]
    slots = 2 * reach + 1
    assert rows == BLOCK and n_head % 2 == 0 and GROUP % (2 * heads) == 0
    exponents = -2.0 * np.repeat(np.arange(dh // 2), 2) / dh
    freq = jnp.asarray((ROPE_BASE**exponents).astype(np.float32)[None, :])
    bf16, f32 = jnp.bfloat16, jnp.float32
    dma = pltpu.SemaphoreType.DMA
    hbm = pl.BlockSpec(memory_space=pltpu.HBM)
    return pl.pallas_call(
        functools.partial(attend, reach, n_ctx, n_head),
        out_shape=jax.ShapeDtypeStruct((rows // n_head, n_head * heads * dh), bf16),
        in_specs=[hbm] * 8,
        out_specs=hbm,
        scratch_shapes=[
            pltpu.SMEM(block_lists.shape, jnp.int32),
            pltpu.SMEM(scale_index.shape, jnp.int32),
            pltpu.SMEM(scale_table.shape, f32),
            pltpu.VMEM((1, rows), jnp.int32),
            pltpu.VMEM((1, dh), f32),
            pltpu.VMEM((rows * heads, dh), bf16),
            pltpu.VMEM((keys, dh), bf16),
            pltpu.VMEM((keys, dh), bf16),
            pltpu.VMEM((rows * heads, dh), f32),
            pltpu.VMEM((heads, rows, dh), bf16),
            pltpu.VMEM((slots * kblocks, BLOCK, dh), bf16),
            pltpu.VMEM((slots * kblocks, dh, BLOCK), bf16),
            pltpu.VMEM((heads, nsel * BLOCK, rows), bf16),
            pltpu.VMEM((heads, 1, rows), f32),
            pltpu.VMEM((heads, n_head, rows // n_head, dh), bf16),
            dma((8,)),
            dma((slots, PIECES)),
            dma((slots, PIECES)),
            dma((slots, CUTS)),
            dma((slots, CUTS)),
            dma((slots, PIECES)),
            dma((slots, PIECES)),
            dma((slots, CUTS)),
            dma((slots, CUTS)),
            dma((heads, n_head - 1)),
            dma((heads, n_head - 1)),
            dma((heads,)),
        ],
        compiler_params=pltpu.CompilerParams(
            collective_id=0, has_side_effects=True, vmem_limit_bytes=67043328
        ),
        name="attend",
    )(
        block_lists,
        scale_index,
        scale_table,
        positions.reshape(1, rows),
        freq,
        queries.reshape(rows * heads, dh),
        key_codes,
        value_codes,
    )


def solution(mesh):
    placed = (
        P(("groups", "ctx"), "head", None),
        P(("groups", "ctx")),
        P("groups", "ctx", None),
        P("groups", "ctx", None),
        P("groups", None, "ctx"),
        P(),
        P(("groups", "head"), None, None),
    )
    return jax.shard_map(
        on_device,
        mesh=mesh,
        in_specs=placed,
        out_specs=P(("groups", "ctx", "head"), None),
        check_vma=False,
    )
```

profile of v0, /device:TPU:0, one launch (start us, length us, event | category | flops | bytes accessed | tf_op | source)
XLA Modules:
  0.0 25.1 jit_solution(14081653101769020725)
XLA Ops:
  0.0 23.4 %attend.1 = bf16[32,4096]{1,0:T(8,128)(2,1)} custom-call(s32[8,4,8]{2,1,0:T(4,128)} %lists_hbm.1, s32[2,2,8]{2,1,0:T(2,128)} %index_hbm.1, f32[2,16]{1,0:T(2,128)} %table_hbm.1, s32[1,128]{1,0:T(1,128)} %bitcast.3, f32[1,128]{1,0:T(1,128)} %constant.2.clone.freq_hbm, bf16[1024,128]{1,0:T(8,128)(2,1)} %bitcast.2, bf16[2,1024,128]{2,1,0:T(8,128)(2,1)} %k_hbm.1, ...), custom_call_target="tpu_custom_call" | custom-call | tf_op jit(solution)/shard_map/attend/pallas_call | solution.py:260
  23.5 1.7 %copy.10 = bf16[32,4096]{1,0:T(8,128)(2,1)} copy(bf16[32,4096]{1,0:T(8,128)(2,1)} %attend.1) | data formatting | bytes 524288
where the time goes:
time: 25.3 us; the launch traced here: 25.1 us
  Pallas kernels  23.4 us (92%)
  local copies, waits for them, and re-layouts  1.67 us (7%)
    pallas_call x1, Pallas kernels, on_device(): pl.pallas_call(functools.partial(attend, reach, n_ctx, n_head), out_shape...  23.4 us
    unnamed x1, local copies, waits for them, and re-layouts  1.67 us

commit v1 on v0

--- a/solution.py
+++ b/solution.py
@@ -259,9 +259,9 @@
     hbm = pl.BlockSpec(memory_space=pltpu.HBM)
     return pl.pallas_call(
         functools.partial(attend, reach, n_ctx, n_head),
-        out_shape=jax.ShapeDtypeStruct((rows // n_head, n_head * heads * dh), bf16),
+        out_shape=pltpu.VMEM((rows // n_head, n_head * heads * dh), bf16),
         in_specs=[hbm] * 8,
-        out_specs=hbm,
+        out_specs=pl.BlockSpec(memory_space=pltpu.VMEM),
         scratch_shapes=[
             pltpu.SMEM(block_lists.shape, jnp.int32),
             pltpu.SMEM(scale_index.shape, jnp.int32),
@@ -292,7 +292,7 @@
             dma((heads,)),
         ],
         compiler_params=pltpu.CompilerParams(
-            collective_id=0, has_side_effects=True, vmem_limit_bytes=67043328
+            collective_id=0, has_side_effects=True, vmem_limit_bytes=67043328 - 2 * rows * heads * dh
         ),
         name="attend",
     )(

time: 25.3 us -> 24.2 us (0.957)
  local copies, waits for them, and re-layouts: 1.67 us -> 0.71 us
    unnamed x1, local copies, waits for them, and re-layouts: 1.67 us -> 0.71 us
where the time goes in v1:
time: 24.2 us; the launch traced here: 24 us
  Pallas kernels  23.3 us (96%)
  local copies, waits for them, and re-layouts  0.71 us (3%)
    pallas_call x1, Pallas kernels, on_device(): pl.pallas_call(functools.partial(attend, reach, n_ctx, n_head), out_shape...  23.3 us
    unnamed x1, local copies, waits for them, and re-layouts  0.71 us

profile of v1, /device:TPU:0, one launch (start us, length us, event | category | flops | bytes accessed | tf_op | source)
XLA Modules:
  0.0 24.0 jit_solution(17650574489664703485)
XLA Ops:
  0.0 23.3 %attend.1 = bf16[32,4096]{1,0:T(8,128)(2,1)S(1)} custom-call(s32[8,4,8]{2,1,0:T(4,128)} %lists_hbm.1, s32[2,2,8]{2,1,0:T(2,128)} %index_hbm.1, f32[2,16]{1,0:T(2,128)} %table_hbm.1, s32[1,128]{1,0:T(1,128)} %bitcast.3, f32[1,128]{1,0:T(1,128)} %constant.2.clone.freq_hbm, bf16[1024,128]{1,0:T(8,128)(2,1)} %bitcast.2, bf16[2,1024,128]{2,1,0:T(8,128)(2,1)} %k_hbm.1, ...), custom_call_target="tpu_custom_call" | custom-call | tf_op jit(solution)/shard_map/attend/pallas_call | solution.py:260
  23.3 0.7 %copy.10 = bf16[32,4096]{1,0:T(8,128)(2,1)} copy(bf16[32,4096]{1,0:T(8,128)(2,1)S(1)} %attend.1) | data formatting | bytes 524288

commit v2 on v1

v2 whole, which is shorter than its diff:
```python
import functools
import math

import jax
import jax.numpy as jnp
import numpy as np
from jax import lax
from jax.experimental import pallas as pl
from jax.experimental.pallas import tpu as pltpu
from jax.sharding import PartitionSpec as P

GROUP = 16
BLOCK = 128
ROPE_BASE = 500000.0
CUTS = (2, 2)
BUNCHES = 1
MESH = pl.DeviceIdType.MESH


def attend(
    reach, n_ctx, n_head,
    lists_hbm, index_hbm, table_hbm, pos_hbm, freq_hbm, q_hbm, k_hbm, v_hbm,
    out_ref,
    lists_s, index_s, table_s, pos_ref, freq_ref,
    qcode, kcode, vcode, qwide, qrot, kbuf, vbuf, wbuf, lbuf, obuf, stage,
    load_sem, isend, irecv, ksend, krecv, vsend, vrecv, kfs, kfr, vfs, vfr, osend, orecv,
    ctx_in, head_in,
):
    c = lax.axis_index("ctx")
    hp = lax.axis_index("head")
    heads, rows, dh = qrot.shape
    kblocks = kcode.shape[1]
    nsel = lists_s.shape[2]
    rows_per = out_ref.shape[0]
    slots = 2 * reach + 1
    half = lax.rem(hp, 2)
    sib = hp + 1 - 2 * half
    kv_head = hp * heads // GROUP

    offsets = [o for d in range(1, reach + 1) for o in (d, -d)]
    others = range(1, n_head)

    def ctx_of(o):
        return lax.rem(c + o + n_ctx, n_ctx)

    def head_of(k):
        return lax.rem(hp + k, n_head)

    def rank(h):
        return h + 1 - 2 * lax.rem(h, 2)

    barrier = pltpu.get_barrier_semaphore()
    greeted = rank(hp)
    for o in offsets:
        greeted += (ctx_of(o) < c).astype(jnp.int32)

        @pl.when(ctx_of(o) > c)
        def _():
            pl.semaphore_signal(barrier, inc=1, device_id={"ctx": ctx_of(o)}, device_id_type=MESH)

    for k in others:

        @pl.when(rank(head_of(k)) > rank(hp))
        def _():
            pl.semaphore_signal(barrier, inc=1, device_id={"head": head_of(k)}, device_id_type=MESH)

    k_load = pltpu.make_async_copy(k_hbm.at[kv_head], kcode.at[reach], load_sem.at[0])
    v_load = pltpu.make_async_copy(v_hbm.at[kv_head], vcode, load_sem.at[1])
    q_load = pltpu.make_async_copy(q_hbm, qcode, load_sem.at[2])
    small = [
        pltpu.make_async_copy(src, dst, load_sem.at[3 + i])
        for i, (src, dst) in enumerate(
            [
                (index_hbm, index_s.at[reach]),
                (table_hbm, table_s),
                (lists_hbm, lists_s),
                (pos_hbm, pos_ref),
                (freq_hbm, freq_ref),
            ]
        )
    ]
    v_load.start()
    for copy in small:
        copy.start()
    k_load.start()
    q_load.start()

    own = reach * kblocks
    part = kblocks // 2
    cuts = len(vbuf)
    wides = [ref.shape[1] for ref in vbuf]
    firsts = [sum(wides[:piece]) for piece in range(cuts)]

    def i_copy(o):
        return pltpu.make_async_remote_copy(
            src_ref=index_hbm,
            dst_ref=index_s.at[reach - o],
            send_sem=isend.at[reach - o],
            recv_sem=irecv.at[reach - o],
            device_id={"ctx": ctx_of(o)},
            device_id_type=MESH,
        )

    def k_copy(o):
        return pltpu.make_async_remote_copy(
            src_ref=k_hbm.at[kv_head, pl.ds(half * part, part)],
            dst_ref=kcode.at[reach - o, pl.ds(half * part, part)],
            send_sem=ksend.at[reach - o],
            recv_sem=krecv.at[reach - o],
            device_id={"ctx": ctx_of(o)},
            device_id_type=MESH,
        )

    def v_copy(o, piece):
        return pltpu.make_async_remote_copy(
            src_ref=vbuf[piece].at[pl.ds(own + half * part, part)],
            dst_ref=vbuf[piece].at[
                pl.ds((reach - o) * kblocks + half * part, part)
            ],
            send_sem=vsend.at[reach - o, piece],
            recv_sem=vrecv.at[reach - o, piece],
            device_id={"ctx": ctx_of(o)},
            device_id_type=MESH,
        )

    def k_forward(slot, which):
        region = kcode.at[slot, pl.ds(which * part, part)]
        return forward(region, kfs.at[slot], kfr.at[slot])

    def v_forward(slot, piece, which):
        region = vbuf[piece].at[pl.ds(slot * kblocks + which * (part), part)]
        return forward(region, vfs.at[slot, piece], vfr.at[slot, piece])

    def forward(region, send, recv):
        return pltpu.make_async_remote_copy(
            src_ref=region,
            dst_ref=region,
            send_sem=send,
            recv_sem=recv,
            device_id={"head": sib},
            device_id_type=MESH,
        )

    def start_keys(o):
        k_copy(o).start()
        i_copy(o).start()

    def start_values(o):
        for piece in range(cuts):
            v_copy(o, piece).start()

    def on_core(which, order, lower, step):
        for o in order:
            side = ctx_of(o) < c if lower else ctx_of(o) > c
            pl.when(jnp.logical_and(half == which, side))(functools.partial(step, o))

    @pl.when(greeted > 0)
    def _():
        pl.semaphore_wait(barrier, greeted)

    on_core(0, offsets, True, start_keys)
    on_core(1, offsets, True, start_keys)
    for o in offsets:

        @pl.when(ctx_of(o) < c)
        def _():
            pl.semaphore_signal(
                ctx_in.at[reach - o], inc=1, device_id={"ctx": ctx_of(o)}, device_id_type=MESH
            )

    for k in others:

        @pl.when(rank(head_of(k)) < rank(hp))
        def _():
            pl.semaphore_signal(
                head_in.at[n_head - k - 1], inc=1, device_id={"head": head_of(k)}, device_id_type=MESH
            )

    def greet_head(k):
        @pl.when(rank(head_of(k)) > rank(hp))
        def _():
            pl.semaphore_wait(head_in.at[k - 1], 1)

    def scale_key(slot, b):
        s = table_s[0, index_s[slot, 0, kv_head, b]]
        kbuf[slot * kblocks + b] = (kcode[slot, b].astype(jnp.float32) * s).astype(jnp.bfloat16)

    v_load.wait()
    for copy in small[:2]:
        copy.wait()
    for b in range(kblocks):
        s = table_s[1, index_s[reach, 1, kv_head, b]]
        rounded = (vcode[b * BLOCK : (b + 1) * BLOCK, :].astype(jnp.float32) * s).astype(jnp.bfloat16)
        turned = rounded.astype(jnp.float32).T
        for piece in range(cuts):
            first, wide = firsts[piece], wides[piece]
            vbuf[piece][own + b] = turned[first : first + wide, :].astype(jnp.bfloat16)
    on_core(0, offsets, True, start_values)
    on_core(1, offsets, True, start_values)

    k_load.wait()
    for b in range(kblocks):
        scale_key(reach, b)

    def greet_keys(o):
        pl.semaphore_wait(ctx_in.at[reach + o], 1)
        start_keys(o)

    def greet_both(o):
        greet_keys(o)
        start_values(o)

    on_core(0, offsets, False, greet_both)
    on_core(1, offsets, False, greet_keys)
    on_core(1, offsets[::-1], False, start_values)

    q_load.wait()
    for copy in small[2:]:
        copy.wait()
    qwide[...] = qcode[...].astype(jnp.float32)
    pos = jnp.broadcast_to(pos_ref[...].astype(jnp.float32), (rows, rows)).T
    angle = pos * freq_ref[...]
    lane = lax.broadcasted_iota(jnp.int32, (rows, dh), 1)
    even = lax.rem(lane, 2) == 0
    cosine = jnp.cos(angle)
    sine = jnp.sin(angle)
    sine = jnp.where(even, -sine, sine)
    for h in range(heads):
        x = qwide[pl.ds(h, rows, stride=heads), :]
        other = jnp.where(even, pltpu.roll(x, dh - 1, 1), pltpu.roll(x, 1, 1))
        qrot[h] = (x * cosine + other * sine).astype(jnp.bfloat16)

    for k in others:
        greet_head(k)
    for o in offsets:
        k_copy(o).wait_recv()
        k_forward(reach - o, half).start()
        i_copy(o).wait_recv()
        for b in range(part):
            scale_key(reach - o, half * part + b)
    for o in offsets:
        k_forward(reach - o, 1 - half).wait_recv()
        for b in range(part):
            scale_key(reach - o, (1 - half) * part + b)

    total = n_ctx * kblocks
    base = total - (c - reach) * kblocks
    factor = math.log2(math.e) / math.sqrt(dh)

    def block_of(h, j):
        return jnp.minimum(lax.rem(lists_s[h, c, j] + base, total), slots * kblocks - 1)

    def score(h, carry):
        gathered = jnp.concatenate([kbuf[block_of(h, j)] for j in range(nsel)], axis=0)
        s = lax.dot_general(
            gathered, qrot[h], (((1,), (1,)), ((), ())), preferred_element_type=jnp.float32
        )
        m = jnp.max(s, axis=0, keepdims=True)
        w = jnp.exp2((s - m) * factor)
        lbuf[h] = 1.0 / jnp.sum(w, axis=0, keepdims=True)
        wbuf[h] = w.astype(jnp.bfloat16)
        return carry

    lax.fori_loop(0, heads, score, 0, unroll=True)

    def o_copy(piece, bunch, k):
        peer = head_of(k)
        size = obuf[piece].shape[1] // BUNCHES
        region = pl.ds(bunch * size, size)
        return pltpu.make_async_remote_copy(
            src_ref=obuf[piece].at[peer, region],
            dst_ref=stage[piece].at[hp, region],
            send_sem=osend.at[piece, bunch, k - 1],
            recv_sem=orecv.at[piece, bunch, k - 1],
            device_id={"head": peer},
            device_id_type=MESH,
        )

    def value(piece, g):
        pack = dh // wides[piece]
        parts = []
        for h in range(g * pack, (g + 1) * pack):
            gathered = jnp.concatenate([vbuf[piece][block_of(h, j)] for j in range(nsel)], axis=1)
            o = jnp.dot(gathered, wbuf[h], preferred_element_type=jnp.float32)
            parts.append(o * lbuf[h])
        t = jnp.concatenate(parts, axis=0).T
        for p in range(n_head):
            obuf[piece][p, g] = t[p * rows_per : (p + 1) * rows_per, :].astype(jnp.bfloat16)

    out_lane = lax.broadcasted_iota(jnp.int32, (rows_per, dh), 1)

    def place(piece, source, ref):
        first, wide = firsts[piece], wides[piece]
        pack = dh // wide
        ours = jnp.logical_and(out_lane >= first, out_lane < first + wide)
        for g in range(ref.shape[0]):
            tile = ref[g].astype(jnp.float32)
            for i in range(pack):
                where = pl.ds(pl.multiple_of((source * heads + g * pack + i) * dh, dh), dh)
                shift = (first - i * wide) % dh
                moved = pltpu.roll(tile, shift, 1) if shift else tile
                if piece:
                    moved = jnp.where(ours, moved, out_ref[:, where].astype(jnp.float32))
                out_ref[:, where] = moved.astype(jnp.bfloat16)

    def pass_on(piece):
        for o in offsets:
            v_copy(o, piece).wait_recv()
            v_forward(reach - o, piece, half).start()

    pass_on(0)
    for piece in range(cuts):
        if piece + 1 < cuts:
            pass_on(piece + 1)
        for o in offsets:
            v_forward(reach - o, piece, 1 - half).wait_recv()
        groups = obuf[piece].shape[1]
        for bunch in range(BUNCHES):
            for g in range(groups // BUNCHES * bunch, groups // BUNCHES * (bunch + 1)):
                value(piece, g)
            for k in others:
                o_copy(piece, bunch, k).start()

    for piece in range(cuts):
        place(piece, hp, obuf[piece].at[hp])

    for o in offsets:
        i_copy(o).wait_send()
        k_copy(o).wait_send()
        k_forward(reach - o, half).wait_send()
        for piece in range(cuts):
            v_copy(o, piece).wait_send()
            v_forward(reach - o, piece, half).wait_send()

    for piece in range(cuts):
        for k in range(1, n_head):
            source = lax.rem(hp - k + n_head, n_head)
            for bunch in range(BUNCHES):
                o_copy(piece, bunch, k).wait_recv()
            place(piece, source, stage[piece].at[source])
    for piece in range(cuts):
        for k in range(1, n_head):
            for bunch in range(BUNCHES):
                o_copy(piece, bunch, k).wait_send()


def on_device(queries, positions, key_codes, value_codes, scale_index, scale_table, block_lists):
    n_ctx = lax.axis_size("ctx")
    n_head = lax.axis_size("head")
    reach = min(3, (n_ctx - 1) // 2)
    rows, heads, dh = queries.shape
    keys = key_codes.shape[1]
    kblocks = keys // BLOCK
    coded = key_codes.reshape(key_codes.shape[0], kblocks, BLOCK, dh)
    nsel = block_lists.shape[2]
    slots = 2 * reach + 1
    assert rows == BLOCK and n_head % 2 == 0 and GROUP % (2 * heads) == 0
    exponents = -2.0 * np.repeat(np.arange(dh // 2), 2) / dh
    freq = jnp.asarray((ROPE_BASE**exponents).astype(np.float32)[None, :])
    bf16, f32 = jnp.bfloat16, jnp.float32
    dma = pltpu.SemaphoreType.DMA
    hbm = pl.BlockSpec(memory_space=pltpu.HBM)
    return pl.pallas_call(
        functools.partial(attend, reach, n_ctx, n_head),
        out_shape=pltpu.VMEM((rows // n_head, n_head * heads * dh), bf16),
        in_specs=[hbm] * 8,
        out_specs=pl.BlockSpec(memory_space=pltpu.VMEM),
        scratch_shapes=[
            pltpu.SMEM(block_lists.shape, jnp.int32),
            pltpu.SMEM((slots,) + scale_index.shape, jnp.int32),
            pltpu.SMEM(scale_table.shape, f32),
            pltpu.VMEM((1, rows), jnp.int32),
            pltpu.VMEM((1, dh), f32),
            pltpu.VMEM((rows * heads, dh), bf16),
            pltpu.VMEM((slots, kblocks, BLOCK, dh), bf16),
            pltpu.VMEM((keys, dh), bf16),
            pltpu.VMEM((rows * heads, dh), f32),
            pltpu.VMEM((heads, rows, dh), bf16),
            pltpu.VMEM((slots * kblocks, BLOCK, dh), bf16),
            [pltpu.VMEM((slots * kblocks, dh // cut, BLOCK), bf16) for cut in CUTS],
            pltpu.VMEM((heads, nsel * BLOCK, rows), bf16),
            pltpu.VMEM((heads, 1, rows), f32),
            [pltpu.VMEM((n_head, heads // cut, rows // n_head, dh), bf16) for cut in CUTS],
            [pltpu.VMEM((n_head, heads // cut, rows // n_head, dh), bf16) for cut in CUTS],
            dma((8,)),
            dma((slots,)),
            dma((slots,)),
            dma((slots,)),
            dma((slots,)),
            dma((slots, len(CUTS))),
            dma((slots, len(CUTS))),
            dma((slots,)),
            dma((slots,)),
            dma((slots, len(CUTS))),
            dma((slots, len(CUTS))),
            dma((len(CUTS), BUNCHES, n_head - 1)),
            dma((len(CUTS), BUNCHES, n_head - 1)),
            pltpu.SemaphoreType.REGULAR((slots,)),
            pltpu.SemaphoreType.REGULAR((n_head - 1,)),
        ],
        compiler_params=pltpu.CompilerParams(
            collective_id=0, has_side_effects=True, vmem_limit_bytes=67043328 - 2 * rows * heads * dh
        ),
        name="attend",
    )(
        block_lists,
        scale_index,
        scale_table,
        positions.reshape(1, rows),
        freq,
        queries.reshape(rows * heads, dh),
        coded,
        value_codes,
    )


def solution(mesh):
    placed = (
        P(("groups", "ctx"), "head", None),
        P(("groups", "ctx")),
        P("groups", "ctx", None),
        P("groups", "ctx", None),
        P("groups", None, "ctx"),
        P(),
        P(("groups", "head"), None, None),
    )
    return jax.shard_map(
        on_device,
        mesh=mesh,
        in_specs=placed,
        out_specs=P(("groups", "ctx", "head"), None),
        check_vma=False,
    )
```

time: 24.2 us -> 23 us (0.950)
  Pallas kernels: 23.3 us -> 22 us
    pallas_call x1, Pallas kernels: 23.3 us -> 22 us  [on_device(): pl.pallas_call(functools.partial(attend, reach, n_ctx, n_head), out_shape...]
where the time goes in v2:
time: 23 us; the launch traced here: 22.7 us
  Pallas kernels  22 us (96%)
  local copies, waits for them, and re-layouts  0.71 us (3%)
    pallas_call x1, Pallas kernels, on_device(): pl.pallas_call(functools.partial(attend, reach, n_ctx, n_head), out_shape...  22 us
    unnamed x1, local copies, waits for them, and re-layouts  0.71 us

profile of v2, /device:TPU:0, one launch (start us, length us, event | category | flops | bytes accessed | tf_op | source)
XLA Modules:
  0.0 22.7 jit_solution(11454036415318200621)
XLA Ops:
  0.0 22.0 %attend.1 = bf16[32,4096]{1,0:T(8,128)(2,1)S(1)} custom-call(s32[8,4,8]{2,1,0:T(4,128)} %lists_hbm.1, s32[2,2,8]{2,1,0:T(2,128)} %index_hbm.1, f32[2,16]{1,0:T(2,128)} %table_hbm.1, s32[1,128]{1,0:T(1,128)} %bitcast.5, f32[1,128]{1,0:T(1,128)} %constant.2.clone.freq_hbm, bf16[1024,128]{1,0:T(8,128)(2,1)} %bitcast.4, bf16[2,8,128,128]{3,2,1,0:T(8,128)(2,1)} %bitcast.3, ...), custom_call_target="tpu_custom_call" | custom-call | tf_op jit(solution)/shard_map/attend/pallas_call | solution.py:363
  22.0 0.7 %copy.10 = bf16[32,4096]{1,0:T(8,128)(2,1)} copy(bf16[32,4096]{1,0:T(8,128)(2,1)S(1)} %attend.1) | data formatting | bytes 524288

commit v3 on v2

--- a/solution.py
+++ b/solution.py
@@ -47,7 +47,7 @@
         return lax.rem(hp + k, n_head)
 
     def rank(h):
-        return h + 1 - 2 * lax.rem(h, 2)
+        return n_head - 1 - h
 
     barrier = pltpu.get_barrier_semaphore()
     greeted = rank(hp)
@@ -149,6 +149,9 @@
         for piece in range(cuts):
             v_copy(o, piece).start()
 
+    def start_value(piece, o):
+        v_copy(o, piece).start()
+
     def on_core(which, order, lower, step):
         for o in order:
             side = ctx_of(o) < c if lower else ctx_of(o) > c
@@ -210,9 +213,11 @@
         greet_keys(o)
         start_values(o)
 
-    on_core(0, offsets, False, greet_both)
+    on_core(0, offsets, False, greet_keys)
     on_core(1, offsets, False, greet_keys)
-    on_core(1, offsets[::-1], False, start_values)
+    for piece in range(cuts):
+        on_core(0, offsets, False, functools.partial(start_value, piece))
+        on_core(1, offsets, False, functools.partial(start_value, piece))
 
     q_load.wait()
     for copy in small[2:]:

time: 23 us -> 22.5 us (0.978)
  Pallas kernels: 22 us -> 21.6 us
    pallas_call x1, Pallas kernels: 22 us -> 21.6 us  [on_device(): pl.pallas_call(functools.partial(attend, reach, n_ctx, n_head), out_shape...]
where the time goes in v3:
time: 22.5 us; the launch traced here: 22.3 us
  Pallas kernels  21.6 us (96%)
  local copies, waits for them, and re-layouts  0.71 us (3%)
    pallas_call x1, Pallas kernels, on_device(): pl.pallas_call(functools.partial(attend, reach, n_ctx, n_head), out_shape...  21.6 us
    unnamed x1, local copies, waits for them, and re-layouts  0.71 us

profile of v3, /device:TPU:0, one launch (start us, length us, event | category | flops | bytes accessed | tf_op | source)
XLA Modules:
  0.0 22.3 jit_solution(12583567182626830852)
XLA Ops:
  0.0 21.6 %attend.1 = bf16[32,4096]{1,0:T(8,128)(2,1)S(1)} custom-call(s32[8,4,8]{2,1,0:T(4,128)} %lists_hbm.1, s32[2,2,8]{2,1,0:T(2,128)} %index_hbm.1, f32[2,16]{1,0:T(2,128)} %table_hbm.1, s32[1,128]{1,0:T(1,128)} %bitcast.5, f32[1,128]{1,0:T(1,128)} %constant.2.clone.freq_hbm, bf16[1024,128]{1,0:T(8,128)(2,1)} %bitcast.4, bf16[2,8,128,128]{3,2,1,0:T(8,128)(2,1)} %bitcast.3, ...), custom_call_target="tpu_custom_call" | custom-call | tf_op jit(solution)/shard_map/attend/pallas_call | solution.py:368
  21.6 0.7 %copy.10 = bf16[32,4096]{1,0:T(8,128)(2,1)} copy(bf16[32,4096]{1,0:T(8,128)(2,1)S(1)} %attend.1) | data formatting | bytes 524288

commit v4 on v3

--- a/solution.py
+++ b/solution.py
@@ -24,7 +24,7 @@
     lists_s, index_s, table_s, pos_ref, freq_ref,
     qcode, kcode, vcode, qwide, qrot, kbuf, vbuf, wbuf, lbuf, obuf, stage,
     load_sem, isend, irecv, ksend, krecv, vsend, vrecv, kfs, kfr, vfs, vfr, osend, orecv,
-    ctx_in, head_in,
+    ctx_in, head_in, row_in,
 ):
     c = lax.axis_index("ctx")
     hp = lax.axis_index("head")
@@ -49,8 +49,11 @@
     def rank(h):
         return n_head - 1 - h
 
+    def direct(k):
+        return jnp.logical_or(c == 0, head_of(k) == sib)
+
     barrier = pltpu.get_barrier_semaphore()
-    greeted = rank(hp)
+    greeted = jnp.int32(0)
     for o in offsets:
         greeted += (ctx_of(o) < c).astype(jnp.int32)
 
@@ -59,8 +62,9 @@
             pl.semaphore_signal(barrier, inc=1, device_id={"ctx": ctx_of(o)}, device_id_type=MESH)
 
     for k in others:
-
-        @pl.when(rank(head_of(k)) > rank(hp))
+        greeted += jnp.logical_and(direct(k), rank(head_of(k)) < rank(hp)).astype(jnp.int32)
+
+        @pl.when(jnp.logical_and(direct(k), rank(head_of(k)) > rank(hp)))
         def _():
             pl.semaphore_signal(barrier, inc=1, device_id={"head": head_of(k)}, device_id_type=MESH)
 
@@ -173,16 +177,31 @@
 
     for k in others:
 
-        @pl.when(rank(head_of(k)) < rank(hp))
+        @pl.when(jnp.logical_and(direct(k), rank(head_of(k)) < rank(hp)))
         def _():
             pl.semaphore_signal(
                 head_in.at[n_head - k - 1], inc=1, device_id={"head": head_of(k)}, device_id_type=MESH
             )
 
     def greet_head(k):
-        @pl.when(rank(head_of(k)) > rank(hp))
+        @pl.when(jnp.logical_or(jnp.logical_not(direct(k)), rank(head_of(k)) > rank(hp)))
         def _():
             pl.semaphore_wait(head_in.at[k - 1], 1)
+
+    def tell_row(k):
+        @pl.when(jnp.logical_and(c + 1 < n_ctx, head_of(k) != sib))
+        def _():
+            pl.semaphore_signal(
+                row_in.at[n_head - k - 1], inc=1, device_id={"head": head_of(k)}, device_id_type=MESH
+            )
+
+    def tell_next(k):
+        @pl.when(jnp.logical_and(c + 1 < n_ctx, head_of(k) != sib))
+        def _():
+            pl.semaphore_wait(row_in.at[k - 1], 1)
+            pl.semaphore_signal(
+                head_in.at[k - 1], inc=1, device_id={"ctx": ctx_of(1)}, device_id_type=MESH
+            )
 
     def scale_key(slot, b):
         s = table_s[0, index_s[slot, 0, kv_head, b]]
@@ -235,8 +254,9 @@
         other = jnp.where(even, pltpu.roll(x, dh - 1, 1), pltpu.roll(x, 1, 1))
         qrot[h] = (x * cosine + other * sine).astype(jnp.bfloat16)
 
-    for k in others:
-        greet_head(k)
+    for step in (greet_head, tell_row, tell_next):
+        for k in others:
+            step(k)
     for o in offsets:
         k_copy(o).wait_recv()
         k_forward(reach - o, half).start()
@@ -402,6 +422,7 @@
             dma((len(CUTS), BUNCHES, n_head - 1)),
             pltpu.SemaphoreType.REGULAR((slots,)),
             pltpu.SemaphoreType.REGULAR((n_head - 1,)),
+            pltpu.SemaphoreType.REGULAR((n_head - 1,)),
         ],
         compiler_params=pltpu.CompilerParams(
             collective_id=0, has_side_effects=True, vmem_limit_bytes=67043328 - 2 * rows * heads * dh

time: 22.5 us -> 22.5 us (level)
  no operation moved by 1% of the time
where the time goes in v4:
time: 22.5 us; the launch traced here: 22.4 us
  Pallas kernels  21.6 us (96%)
  local copies, waits for them, and re-layouts  0.71 us (3%)
    pallas_call x1, Pallas kernels, on_device(): pl.pallas_call(functools.partial(attend, reach, n_ctx, n_head), out_shape...  21.6 us
    unnamed x1, local copies, waits for them, and re-layouts  0.71 us

profile of v4, /device:TPU:0, one launch (start us, length us, event | category | flops | bytes accessed | tf_op | source)
XLA Modules:
  0.0 22.4 jit_solution(16984509767172598206)
XLA Ops:
  0.0 21.6 %attend.1 = bf16[32,4096]{1,0:T(8,128)(2,1)S(1)} custom-call(s32[8,4,8]{2,1,0:T(4,128)} %lists_hbm.1, s32[2,2,8]{2,1,0:T(2,128)} %index_hbm.1, f32[2,16]{1,0:T(2,128)} %table_hbm.1, s32[1,128]{1,0:T(1,128)} %bitcast.5, f32[1,128]{1,0:T(1,128)} %constant.2.clone.freq_hbm, bf16[1024,128]{1,0:T(8,128)(2,1)} %bitcast.4, bf16[2,8,128,128]{3,2,1,0:T(8,128)(2,1)} %bitcast.3, ...), custom_call_target="tpu_custom_call" | custom-call | tf_op jit(solution)/shard_map/attend/pallas_call | solution.py:388
  21.6 0.7 %copy.10 = bf16[32,4096]{1,0:T(8,128)(2,1)} copy(bf16[32,4096]{1,0:T(8,128)(2,1)S(1)} %attend.1) | data formatting | bytes 524288

commit v5 on v4

--- a/solution.py
+++ b/solution.py
@@ -358,7 +358,8 @@
             v_forward(reach - o, piece, half).wait_send()
 
     for piece in range(cuts):
-        for k in range(1, n_head):
+        for turn in range(n_head - 1):
+            k = 1 + lax.rem(turn + (n_head - 2) * (1 - half), n_head - 1)
             source = lax.rem(hp - k + n_head, n_head)
             for bunch in range(BUNCHES):
                 o_copy(piece, bunch, k).wait_recv()

time: 22.5 us -> 22.4 us (level)
  no operation moved by 1% of the time
where the time goes in v5:
time: 22.4 us; the launch traced here: 22.3 us
  Pallas kernels  21.6 us (96%)
  local copies, waits for them, and re-layouts  0.71 us (3%)
    pallas_call x1, Pallas kernels, on_device(): pl.pallas_call(functools.partial(attend, reach, n_ctx, n_head), out_shape...  21.6 us
    unnamed x1, local copies, waits for them, and re-layouts  0.71 us

profile of v5, /device:TPU:0, one launch (start us, length us, event | category | flops | bytes accessed | tf_op | source)
XLA Modules:
  0.0 22.3 jit_solution(5046099996656667849)
XLA Ops:
  0.0 21.6 %attend.1 = bf16[32,4096]{1,0:T(8,128)(2,1)S(1)} custom-call(s32[8,4,8]{2,1,0:T(4,128)} %lists_hbm.1, s32[2,2,8]{2,1,0:T(2,128)} %index_hbm.1, f32[2,16]{1,0:T(2,128)} %table_hbm.1, s32[1,128]{1,0:T(1,128)} %bitcast.5, f32[1,128]{1,0:T(1,128)} %constant.2.clone.freq_hbm, bf16[1024,128]{1,0:T(8,128)(2,1)} %bitcast.4, bf16[2,8,128,128]{3,2,1,0:T(8,128)(2,1)} %bitcast.3, ...), custom_call_target="tpu_custom_call" | custom-call | tf_op jit(solution)/shard_map/attend/pallas_call | solution.py:389
  21.6 0.7 %copy.10 = bf16[32,4096]{1,0:T(8,128)(2,1)} copy(bf16[32,4096]{1,0:T(8,128)(2,1)S(1)} %attend.1) | data formatting | bytes 524288

commit v6 on v4

--- a/solution.py
+++ b/solution.py
@@ -220,10 +220,6 @@
     on_core(0, offsets, True, start_values)
     on_core(1, offsets, True, start_values)
 
-    k_load.wait()
-    for b in range(kblocks):
-        scale_key(reach, b)
-
     def greet_keys(o):
         pl.semaphore_wait(ctx_in.at[reach + o], 1)
         start_keys(o)
@@ -237,6 +233,10 @@
     for piece in range(cuts):
         on_core(0, offsets, False, functools.partial(start_value, piece))
         on_core(1, offsets, False, functools.partial(start_value, piece))
+
+    k_load.wait()
+    for b in range(kblocks):
+        scale_key(reach, b)
 
     q_load.wait()
     for copy in small[2:]:

time: 22.5 us -> 22.5 us (level)
  no operation moved by 1% of the time
where the time goes in v6:
time: 22.5 us; the launch traced here: 22.4 us
  Pallas kernels  21.6 us (96%)
  local copies, waits for them, and re-layouts  0.71 us (3%)
    pallas_call x1, Pallas kernels, on_device(): pl.pallas_call(functools.partial(attend, reach, n_ctx, n_head), out_shape...  21.6 us
    unnamed x1, local copies, waits for them, and re-layouts  0.71 us

profile of v6, /device:TPU:0, one launch (start us, length us, event | category | flops | bytes accessed | tf_op | source)
XLA Modules:
  0.0 22.4 jit_solution(2018268934717783515)
XLA Ops:
  0.0 21.6 %attend.1 = bf16[32,4096]{1,0:T(8,128)(2,1)S(1)} custom-call(s32[8,4,8]{2,1,0:T(4,128)} %lists_hbm.1, s32[2,2,8]{2,1,0:T(2,128)} %index_hbm.1, f32[2,16]{1,0:T(2,128)} %table_hbm.1, s32[1,128]{1,0:T(1,128)} %bitcast.5, f32[1,128]{1,0:T(1,128)} %constant.2.clone.freq_hbm, bf16[1024,128]{1,0:T(8,128)(2,1)} %bitcast.4, bf16[2,8,128,128]{3,2,1,0:T(8,128)(2,1)} %bitcast.3, ...), custom_call_target="tpu_custom_call" | custom-call | tf_op jit(solution)/shard_map/attend/pallas_call | solution.py:388
  21.6 0.7 %copy.10 = bf16[32,4096]{1,0:T(8,128)(2,1)} copy(bf16[32,4096]{1,0:T(8,128)(2,1)S(1)} %attend.1) | data formatting | bytes 524288
